TPU v7x, 32 devices: a whole 2x2x4 slice. The times are simulated.
32 devices in a mesh: dp: 8 (over z, x), mp: 4 (over y, core).
Axes of the slice: x: 2, y: 2, z: 4, core: 2. Of those that a mesh axis runs over, the one named last changes fastest.
Arguments:
- tokens: bfloat16 [256, 48, 3584], P('dp', None, 'mp'), may hold values from -180 to 180
- norm_gain: float32 [3584], replicated, may hold values from 0.1 to 1.9
- w_query: bfloat16 [3584, 3584], P('dp', 'mp'), may hold values from -0.16 to 0.16
- w_keyval: bfloat16 [3584, 2, 512], P('dp', None, 'mp'), may hold values from -0.16 to 0.16
- w_out: bfloat16 [3584, 3584], P('mp', 'dp'), may hold values from -0.09375 to 0.09375
- residents: bfloat16 [8, 2048, 3584], P('dp', 'mp'), may hold values from -6 to 6
- lengths: int32 [256], P('dp'), may hold values from 6 to 48
- cluster: int32 [256, 1], P('dp'), may hold values from 0 to 7; in each aligned block of 32 rows (0 to 31, 32 to 63, ...) at most 4 rows name the same one
- owner: int32 [8], replicated, may hold values from 0 to 7, each once
- counts: int32 [8], replicated, may hold values from 256 to 2048
- flags: int32 [256], P('dp'), may hold values 0 or 1
Outputs:
- similarity: float32 [256, 2048], P('dp', 'mp')
Inputs may be any that keep to these rules, and one draw needn't show every extreme that they name: Each dialogue's cluster; among the 32 dialogues of one index of dp (aligned blocks of rows) no cluster is named more than 4 times. owner gives every cluster a distinct index of dp that holds its residents.
All inputs are finite; a program needn't handle non-finite values. No bound on the sum of `flags` on one device may be relied on, other than what follows from the above.
Results may differ from a plain program's by a relative error of at most 0.013.
Values may be sent and summed in bfloat16 or wider, within the bound.
A program may use at most 128 MiB of HBM per device.

v0:
```python
import math
import jax
import jax.numpy as jnp
from jax import lax
from jax.sharding import PartitionSpec as P

HEAD_DIM = 128
rope_base = 1000000.0
logit_scale = 100.0


def rotate(values, positions):
    half = values.shape[-1] // 2
    freqs = rope_base ** (-jnp.arange(half, dtype=jnp.float32) * 2.0 / values.shape[-1])
    angles = positions.astype(jnp.float32)[:, None] * freqs[None, :]
    cosine = jnp.cos(angles)[:, None, :]
    sine = jnp.sin(angles)[:, None, :]
    first = values[..., :half]
    second = values[..., half:]
    return jnp.concatenate(
        [first * cosine - second * sine, second * cosine + first * sine], axis=-1
    )


def attend(query, keys, values, length):
    seq_len = query.shape[0]
    kv_count = keys.shape[1]
    group = query.shape[1] // kv_count
    grouped = query.reshape(seq_len, kv_count, group, query.shape[-1])
    scores = jnp.einsum(
        "qkgd,pkd->kgqp", grouped, keys, preferred_element_type=jnp.float32
    ) / math.sqrt(query.shape[-1])
    row_pos = jnp.arange(seq_len)[:, None]
    col_pos = jnp.arange(seq_len)[None, :]
    allowed = (col_pos <= row_pos) & (col_pos < length)
    scores = jnp.where(allowed, scores, -1e30)
    highest = jnp.max(scores, axis=-1, keepdims=True)
    expanded = jnp.exp(scores - highest)
    weights = (expanded / jnp.sum(expanded, axis=-1, keepdims=True)).astype(jnp.bfloat16)
    context = jnp.einsum("kgqp,pkd->qkgd", weights, values, preferred_element_type=jnp.float32)
    valid = (jnp.arange(seq_len) < length).astype(jnp.float32)
    pooled = jnp.sum(context * valid[:, None, None, None], axis=0) / length.astype(jnp.float32)
    return pooled.reshape(-1)


def local(
    tokens, norm_gain, w_query, w_keyval, w_out, residents, lengths, cluster, owner, counts, flags
):
    gathered = lax.all_gather(tokens, "mp", axis=2, tiled=True)
    dialogs, seq_len, width = gathered.shape
    hidden = gathered.astype(jnp.float32)
    normed = (
        hidden * lax.rsqrt(jnp.mean(hidden * hidden, axis=-1, keepdims=True) + 1e-06) * norm_gain
    ).astype(jnp.bfloat16)
    normed_flat = normed.reshape(dialogs * seq_len, width)
    query_cols = w_query.shape[1]
    keyval_cols = w_keyval.shape[2]
    pieces = (
        lax.all_gather(w_query, "dp", axis=0, tiled=True),
        lax.all_gather(w_keyval, "dp", axis=0, tiled=True),
    )
    keyval_piece = pieces[1].reshape(pieces[1].shape[0], 2 * keyval_cols)
    query_sum = jnp.dot(normed_flat, pieces[0], preferred_element_type=jnp.float32)
    keyval_sum = jnp.dot(normed_flat, keyval_piece, preferred_element_type=jnp.float32)
    positions = jnp.arange(seq_len)
    local_heads = query_cols // HEAD_DIM
    local_kv = keyval_cols // HEAD_DIM
    query = jax.vmap(lambda block: rotate(block, positions))(
        query_sum.reshape(dialogs, seq_len, local_heads, HEAD_DIM)
    ).astype(jnp.bfloat16)
    keys = jax.vmap(lambda block: rotate(block, positions))(
        keyval_sum[:, :keyval_cols].reshape(dialogs, seq_len, local_kv, HEAD_DIM)
    ).astype(jnp.bfloat16)
    values = (
        keyval_sum[:, keyval_cols:]
        .reshape(dialogs, seq_len, local_kv, HEAD_DIM)
        .astype(jnp.bfloat16)
    )
    pooled_context = jax.vmap(attend)(query, keys, values, lengths).astype(jnp.bfloat16)
    valid = (positions[None, :] < lengths[:, None]).astype(jnp.float32)
    pooled_input = (
        jnp.sum(hidden * valid[:, :, None], axis=1) / lengths.astype(jnp.float32)[:, None]
    )
    partial_out = jnp.dot(
        pooled_context,
        lax.all_gather(w_out, "dp", axis=1, tiled=True),
        preferred_element_type=jnp.float32,
    )
    projected = lax.psum(partial_out.astype(jnp.bfloat16), "mp").astype(jnp.float32)
    embedding = pooled_input + projected
    unit = embedding * lax.rsqrt(jnp.sum(embedding * embedding, axis=-1, keepdims=True) + 1e-06)
    unit = (unit * flags.astype(jnp.float32)[:, None]).astype(jnp.bfloat16)
    my_index = lax.axis_index("dp")
    owner_count = lax.axis_size("dp")
    my_count = jnp.sum(jnp.where(owner == my_index, counts, 0))
    members = residents[0]
    member_count = members.shape[0]
    inverse_norm = lax.rsqrt(
        jnp.einsum("md,md->m", members, members, preferred_element_type=jnp.float32) + 1e-06
    )
    member_start = lax.axis_index("mp") * member_count
    live = member_start + jnp.arange(member_count) < my_count
    table_size = owner.shape[0]
    cluster_ids = cluster[:, 0]
    destination = jnp.sum(
        jnp.where(jnp.arange(table_size)[None, :] == cluster_ids[:, None], owner[None, :], 0),
        axis=1,
    )
    capacity = max(1, -(-dialogs // owner_count))
    order = jnp.arange(dialogs)
    earlier = (destination[None, :] == destination[:, None]) & (order[None, :] < order[:, None])
    rank = jnp.sum(earlier.astype(jnp.int32), axis=1)
    onehot = (jnp.arange(owner_count)[:, None, None] == destination[None, None, :]) & (
        jnp.arange(capacity)[None, :, None] == rank[None, None, :]
    )
    outgoing = jnp.einsum(
        "ocn,nd->ocd", onehot.astype(jnp.bfloat16), unit, preferred_element_type=jnp.float32
    ).astype(jnp.bfloat16)
    query_rows = lax.all_to_all(outgoing, "dp", split_axis=0, concat_axis=0, tiled=True)
    dots = lax.dot_general(
        query_rows,
        members,
        (((query_rows.ndim - 1,), (1,)), ((), ())),
        preferred_element_type=jnp.float32,
    )
    returned = lax.all_to_all(
        jnp.where(live, logit_scale * dots * inverse_norm, 0.0).astype(jnp.bfloat16),
        "dp",
        split_axis=0,
        concat_axis=0,
        tiled=True,
    ).astype(jnp.float32)
    similarity = jnp.einsum(
        "ocn,ocm->nm", onehot.astype(jnp.float32), returned, precision=lax.Precision.HIGHEST
    )
    return similarity


def solution(mesh):
    in_specs = (
        P("dp", None, "mp"),
        P(),
        P("dp", "mp"),
        P("dp", None, "mp"),
        P("mp", "dp"),
        P("dp", "mp", None),
        P("dp"),
        P("dp", None),
        P(),
        P(),
        P("dp"),
    )
    out_specs = P("dp", "mp")
    return jax.shard_map(local, mesh=mesh, in_specs=in_specs, out_specs=out_specs, check_vma=False)
```

profile of v0, /device:TPU:0, one launch (start us, length us, event | category | flops | bytes accessed | tf_op | source)
XLA Modules:
  0.0 408.5 jit_solution(2310838354348667568)
XLA Ops:
  12.9 2.8 fusion.6
  15.7 97.3 %all-gather.9.cloned.1.call-done = bf16[3584,896]{1,0:T(8,128)(2,1)} async-done(((bf16[448,896]{1,0:T(8,128)(2,1)}), bf16[3584,896]{1,0:T(8,128)(2,1)}) %all-gather.9.cloned.1.call-update) | async-done | bytes 6422544 | tf_op jit(solution)/shard_map/all_gather | solution.py:59
  113.0 9.7 %copy.20 = bf16[896,3584]{1,0:T(8,128)(2,1)} copy(bf16[896,3584]{0,1:T(8,128)(2,1)} %bitcast.86) | data formatting | bytes 12845056 | tf_op jit(solution)/shard_map/dot_general | solution.py:63
  122.7 63.2 %all-gather.5.cloned.1.call-done = bf16[32,48,3584]{2,1,0:T(8,128)(2,1)} async-done(((bf16[32,48,896]{2,1,0:T(8,128)(2,1)}), bf16[32,48,3584]{2,1,0:T(8,128)(2,1)}) %all-gather.5.cloned.1.call-update) | async-done | bytes 11010064 | tf_op jit(solution)/shard_map/all_gather | solution.py:49
  185.8 8.9 %fusion = (f32[32,3584]{1,0:T(8,128)S(1)}, f32[32,48]{1,0:T(8,128)S(1)}) fusion(bf16[32,48,3584]{2,1,0:T(8,128)(2,1)} %all-gather.5.cloned.1.call-done, f32[32,48]{1,0:T(8,128)S(1)} %get-tuple-element.14), kind=kLoop, calls=%fused_computation.3 | loop fusion | flops 27408896 | bytes 11481088 | tf_op jit(solution)/shard_map/reduce_sum | solution.py:82
  194.8 11.0 %fusion.3 = bf16[32,48,3584]{2,1,0:T(8,128)(2,1)} fusion(bf16[32,48,3584]{2,1,0:T(8,128)(2,1)} %all-gather.5.cloned.1.call-done, f32[3584]{0:T(1024)S(1)} %copy-done.1, f32[32,48]{1,0:T(8,128)S(1)} %add_rsqrt_fusion), kind=kLoop, calls=%fused_computation.6 | loop fusion | flops 22020096 | bytes 22040576 | tf_op jit(solution)/shard_map/convert_element_type | solution.py:54
  205.7 28.8 %all-gather.7.cloned.1.call-done = bf16[3584,2,128]{2,1,0:T(2,128)(2,1)} async-done(((bf16[448,2,128]{2,1,0:T(2,128)(2,1)}), bf16[3584,2,128]{2,1,0:T(2,128)(2,1)}) %all-gather.7.cloned.1.call-update) | async-done | bytes 1835024 | tf_op jit(solution)/shard_map/all_gather | solution.py:60
  234.5 7.2 %fusion.22 = f32[1536,256]{1,0:T(8,128)S(1)} fusion(bf16[1536,3584]{1,0:T(8,128)(2,1)} %bitcast.84, bf16[448,8,2,128]{3,2,1,0:T(2,128)(2,1)} %bitcast.92), kind=kOutput, calls=%fused_computation.34 | convolution fusion | flops 2818572288 | bytes 14417920 | tf_op jit(solution)/shard_map/dot_general | solution.py:64
  242.4 1.5 slice-done.1
  243.8 11.6 %fusion.4 = f32[32,48,7,128]{3,1,2,0:T(8,128)S(1)} fusion(bf16[7,128,3584,1]{2,1,0,3:T(8,128)(2,1)S(1)} %bitcast.89, bf16[32,48,3584]{2,1,0:T(8,128)(2,1)S(1)} %copy-done), kind=kOutput, calls=%fused_computation.7 | convolution fusion | flops 9865003008 | bytes 22937600 | tf_op jit(solution)/shard_map/dot_general | solution.py:63
  255.5 1.9 subtract_convert_fusion
  257.4 3.6 fusion.9
  261.0 2.1 fusion.8
  263.2 2.3 fusion.7
  265.5 70.8 %all-gather.11.cloned.1.call-done = bf16[896,3584]{0,1:T(8,128)(2,1)} async-done(((bf16[896,448]{0,1:T(8,128)(2,1)}), bf16[896,3584]{0,1:T(8,128)(2,1)}) %all-gather.11.cloned.1.call-update) | async-done | bytes 6422544 | tf_op jit(solution)/shard_map/all_gather | solution.py:86
  336.3 5.5 %convolution_convert_fusion.1 = bf16[32,3584]{1,0:T(8,128)(2,1)} fusion(bf16[896,3584]{0,1:T(8,128)(2,1)} %all-gather.11.cloned.1.call-done, f32[4,8,7,128]{3,2,1,0:T(8,128)S(1)} %bitcast.91, f32[32]{0:T(128)S(1)} %convert_element_type.91), kind=kOutput, calls=%fused_computation.20 | convolution fusion | flops 205692928 | bytes 6766720 | tf_op jit(solution)/shard_map/dot_general | solution.py:84
  341.8 30.2 %all-reduce.2.cloned.1.call-done = bf16[32,3584]{1,0:T(8,128)(2,1)} async-done(((bf16[32,3584]{1,0:T(8,128)(2,1)}), bf16[32,3584]{1,0:T(8,128)(2,1)}) %all-reduce.2.cloned.1.call-update) | async-done | bytes 229392 | tf_op jit(solution)/shard_map/psum | solution.py:89
  372.0 1.2 multiply_reduce_fusion
  373.2 1.9 convolution_convert_fusion
  375.1 5.5 %all-to-all-start = ((bf16[8,4,3584]{2,1,0:T(4,128)(2,1)}), bf16[8,4,3584]{2,1,0:T(4,128)(2,1)S(1)}, u32[]{:S(2)}, u32[]{:S(2)}) async-start(bf16[8,4,3584]{2,1,0:T(4,128)(2,1)} %convolution_convert_fusion), calls=%async_computation | async-start | bytes 458752 | tf_op jit(solution)/shard_map/all_to_all | solution.py:119
  382.0 6.7 %all-to-all-done = bf16[8,4,3584]{2,1,0:T(4,128)(2,1)S(1)} async-done(((bf16[8,4,3584]{2,1,0:T(4,128)(2,1)}), bf16[8,4,3584]{2,1,0:T(4,128)(2,1)S(1)}, u32[]{:S(2)}, u32[]{:S(2)}) %all-to-all-start) | async-done | bytes 229408 | tf_op jit(solution)/shard_map/all_to_all | solution.py:119
  388.7 3.2 fusion.33
  391.9 9.2 %all_to_all.10 = bf16[8,4,512]{2,1,0:T(4,128)(2,1)S(1)} all-to-all(bf16[8,4,512]{2,1,0:T(4,128)(2,1)S(1)} %fusion.33), channel_id=1, replica_groups=mesh['dp'=8,'mp'=4] {'dp'}, dimensions={0} | all-to-all | bytes 65536 | tf_op jit(solution)/shard_map/all_to_all | solution.py:126
  401.2 0.8 convolution_bitcast_fusion
  (43 shorter events, 8.2 us)
Async XLA Ops:
  6.5 106.4 %all-gather.9.cloned.1.call-start = ((), (), s32[]{:S(2)}) async-start(), calls=%async_computation.4 | async-start | bytes 7225344 | tf_op jit(solution)/shard_map/all_gather | solution.py:59
  7.3 178.6 %all-gather.5.cloned.1.call-start = ((), (), s32[]{:S(2)}) async-start(), calls=%async_computation.2 | async-start | bytes 13762560 | tf_op jit(solution)/shard_map/all_gather | solution.py:49
  8.0 226.5 %all-gather.7.cloned.1.call-start = ((), (), s32[]{:S(2)}) async-start(), calls=%async_computation.3 | async-start | bytes 2064384 | tf_op jit(solution)/shard_map/all_gather | solution.py:60
  8.7 327.5 %all-gather.11.cloned.1.call-start = ((), (), s32[]{:S(2)}) async-start(), calls=%async_computation.5 | async-start | bytes 7225344 | tf_op jit(solution)/shard_map/all_gather | solution.py:86
  9.3 362.7 %all-reduce.2.cloned.1.call-start = ((), (), s32[]{:S(2)}) async-start(), calls=%async_computation.6 | async-start | bytes 458752 | tf_op jit(solution)/shard_map/psum | solution.py:89
  185.8 8.9 %copy-start.1 = (f32[3584]{0:T(1024)S(1)}, f32[3584]{0:T(1024)}, u32[]{:S(2)}) copy-start(f32[3584]{0:T(1024)} %param.12) | copy-start | bytes 43012
  194.8 47.4 %slice-start = ((s8[6422528]{0:T(1024)(128)(4,1)}), s8[2228224]{0:T(1024)(128)(4,1)S(1)}, s32[]{:S(2)}) async-start(s8[6422528]{0:T(1024)(128)(4,1)} %bitcast.87), calls=%async_computation.7 | async-start | bytes 4456448
  234.5 7.8 %copy-start = (bf16[32,48,3584]{2,1,0:T(8,128)(2,1)S(1)}, bf16[32,48,3584]{2,1,0:T(8,128)(2,1)}, u32[]{:S(2)}) copy-start(bf16[32,48,3584]{2,1,0:T(8,128)(2,1)} %fusion.3) | copy-start | bytes 33030148
  234.5 9.3 %slice-start.1 = ((s8[6422528]{0:T(1024)(128)(4,1)}), s8[4194304]{0:T(1024)(128)(4,1)S(1)}, s32[]{:S(2)}) async-start(s8[6422528]{0:T(1024)(128)(4,1)} %bitcast.87), calls=%async_computation.8 | async-start | bytes 8388608
  265.5 115.2 %copy-start.2 = (s32[8]{0:T(128)S(1)}, s32[8]{0:T(128)}, u32[]{:S(2)}) copy-start(s32[8]{0:T(128)} %param.19) | copy-start | bytes 100
  265.5 115.2 %copy-start.3 = (s32[8]{0:T(128)S(1)}, s32[8]{0:T(128)}, u32[]{:S(2)}) copy-start(s32[8]{0:T(128)} %param.20) | copy-start | bytes 100
  375.1 13.5 %all-to-all-start = ((bf16[8,4,3584]{2,1,0:T(4,128)(2,1)}), bf16[8,4,3584]{2,1,0:T(4,128)(2,1)S(1)}, u32[]{:S(2)}, u32[]{:S(2)}) async-start(bf16[8,4,3584]{2,1,0:T(4,128)(2,1)} %convolution_convert_fusion), calls=%async_computation | async-start | bytes 458752 | tf_op jit(solution)/shard_map/all_to_all | solution.py:119
Sparse Core Ops, SparseCore 0:
  9.5 103.3 all-gather.8
  114.5 71.2 all-gather.4
  188.0 46.4 all-gather.6
  236.6 99.6 all-gather.10
  341.9 30.0 all-reduce.1
where the time goes:
time: 409 us
  waiting for transfers between devices  299 us (73%)
  matrix products  36.3 us (9%)
  other arithmetic  33 us (8%)
  between operations  13.3 us (3%)
  local copies, waits for them, and re-layouts  11.5 us (3%)
  blocking collectives  9.24 us (2%)
  starting transfers between devices  5.66 us (1%)
    all_gather x1, waiting for transfers between devices, local(): lax.all_gather(w_query, 'dp', axis=0, tiled=True)  97.3 us
    all_gather x1, waiting for transfers between devices, local(): lax.all_gather(w_out, 'dp', axis=1, tiled=True)  70.8 us
    all_gather x1, waiting for transfers between devices, local(): gathered = lax.all_gather(tokens, 'mp', axis=2, tiled=True)  63.2 us
    psum x1, waiting for transfers between devices, local(): lax.psum(partial_out.astype(jnp.bfloat16), 'mp').astype(jnp.float32)  30.2 us
    all_gather x1, waiting for transfers between devices, local(): lax.all_gather(w_keyval, 'dp', axis=0, tiled=True)  28.8 us
    dot_general x1, matrix products, local(): jnp.dot(normed_flat, pieces[0], preferred_element_type=jnp.float32)  11.6 us
    convert_element_type x1, other arithmetic, local(): normed = (hidden * lax.rsqrt(jnp.mean(hidden * hidden, axis=-1, keepdims=...  11 us
    dot_general x1, local copies, waits for them, and re-layouts, local(): jnp.dot(normed_flat, pieces[0], preferred_element_type=jnp.float32)  9.72 us
  transfers between devices with their start and end apart: 6, of which 6 were waited for; matrix products, arithmetic and copies ran while one was open for 16% of the time, Pallas kernels for 0%

commit v1 on v0

--- a/solution.py
+++ b/solution.py
@@ -86,7 +86,9 @@
         lax.all_gather(w_out, "dp", axis=1, tiled=True),
         preferred_element_type=jnp.float32,
     )
-    projected = lax.psum(partial_out.astype(jnp.bfloat16), "mp").astype(jnp.float32)
+    projected = jnp.sum(lax.all_gather(partial_out.astype(jnp.bfloat16), "mp"), axis=0).astype(
+        jnp.float32
+    )
     embedding = pooled_input + projected
     unit = embedding * lax.rsqrt(jnp.sum(embedding * embedding, axis=-1, keepdims=True) + 1e-06)
     unit = (unit * flags.astype(jnp.float32)[:, None]).astype(jnp.bfloat16)

time: 409 us -> 385 us (0.941)
  waiting for transfers between devices: 299 us -> 270 us
  blocking collectives: 9.24 us -> 19.1 us
    psum x1 -> x0, waiting for transfers between devices: 30.2 us -> none  [local(): lax.psum(partial_out.astype(jnp.bfloat16), 'mp').astype(jnp.float32)]
    all_gather x0 -> x1, blocking collectives: none -> 9.31 us  [local(): lax.all_gather(partial_out.astype(jnp.bfloat16), 'mp')]
  transfers between devices with their start and end apart: 6 -> 5, of which waited for: 6 -> 5; matrix products, arithmetic and copies ran while one was open for 16% -> 17% of each run, Pallas kernels for 0% -> 0%
where the time goes in v1:
time: 385 us
  waiting for transfers between devices  270 us (70%)
  matrix products  34.6 us (9%)
  other arithmetic  32.3 us (8%)
  blocking collectives  19.1 us (5%)
  between operations  13.3 us (3%)
  local copies, waits for them, and re-layouts  11.5 us (3%)
    all_gather x1, waiting for transfers between devices, local(): lax.all_gather(w_query, 'dp', axis=0, tiled=True)  97.2 us
    all_gather x1, waiting for transfers between devices, local(): lax.all_gather(w_out, 'dp', axis=1, tiled=True)  70.8 us
    all_gather x1, waiting for transfers between devices, local(): gathered = lax.all_gather(tokens, 'mp', axis=2, tiled=True)  63.2 us
    all_gather x1, waiting for transfers between devices, local(): lax.all_gather(w_keyval, 'dp', axis=0, tiled=True)  28.8 us
    dot_general x1, matrix products, local(): jnp.dot(normed_flat, pieces[0], preferred_element_type=jnp.float32)  11.6 us
    convert_element_type x1, other arithmetic, local(): normed = (hidden * lax.rsqrt(jnp.mean(hidden * hidden, axis=-1, keepdims=...  11 us
    all_to_all x1, blocking collectives, local(): lax.all_to_all(jnp.where(live, logit_scale * dots * inverse_norm, 0.0).as...  9.81 us
    dot_general x1, local copies, waits for them, and re-layouts, local(): jnp.dot(normed_flat, pieces[0], preferred_element_type=jnp.float32)  9.72 us
  transfers between devices with their start and end apart: 5, of which 5 were waited for; matrix products, arithmetic and copies ran while one was open for 17% of the time, Pallas kernels for 0%

profile of v1, /device:TPU:0, one launch (start us, length us, event | category | flops | bytes accessed | tf_op | source)
XLA Modules:
  0.0 384.8 jit_solution(11530685675220997329)
XLA Ops:
  10.7 0.8 select_reduce_fusion
  12.8 2.8 fusion.6
  15.7 97.2 %all-gather.10.cloned.1.call-done = bf16[3584,896]{1,0:T(8,128)(2,1)} async-done(((bf16[448,896]{1,0:T(8,128)(2,1)}), bf16[3584,896]{1,0:T(8,128)(2,1)}) %all-gather.10.cloned.1.call-update) | async-done | bytes 6422544 | tf_op jit(solution)/shard_map/all_gather | solution.py:59
  112.9 9.7 %copy.20 = bf16[896,3584]{1,0:T(8,128)(2,1)} copy(bf16[896,3584]{0,1:T(8,128)(2,1)} %bitcast.87) | data formatting | bytes 12845056 | tf_op jit(solution)/shard_map/dot_general | solution.py:63
  122.6 63.2 %all-gather.6.cloned.1.call-done = bf16[32,48,3584]{2,1,0:T(8,128)(2,1)} async-done(((bf16[32,48,896]{2,1,0:T(8,128)(2,1)}), bf16[32,48,3584]{2,1,0:T(8,128)(2,1)}) %all-gather.6.cloned.1.call-update) | async-done | bytes 11010064 | tf_op jit(solution)/shard_map/all_gather | solution.py:49
  185.8 8.9 %fusion = (f32[32,3584]{1,0:T(8,128)S(1)}, f32[32,48]{1,0:T(8,128)S(1)}) fusion(bf16[32,48,3584]{2,1,0:T(8,128)(2,1)} %all-gather.6.cloned.1.call-done, f32[32,48]{1,0:T(8,128)S(1)} %get-tuple-element.14), kind=kLoop, calls=%fused_computation.3 | loop fusion | flops 27408896 | bytes 11481088 | tf_op jit(solution)/shard_map/reduce_sum | solution.py:82
  194.7 11.0 %fusion.3 = bf16[32,48,3584]{2,1,0:T(8,128)(2,1)} fusion(bf16[32,48,3584]{2,1,0:T(8,128)(2,1)} %all-gather.6.cloned.1.call-done, f32[3584]{0:T(1024)S(1)} %copy-done.1, f32[32,48]{1,0:T(8,128)S(1)} %add_rsqrt_fusion), kind=kLoop, calls=%fused_computation.6 | loop fusion | flops 22020096 | bytes 22040576 | tf_op jit(solution)/shard_map/convert_element_type | solution.py:54
  205.7 28.8 %all-gather.8.cloned.1.call-done = bf16[3584,2,128]{2,1,0:T(2,128)(2,1)} async-done(((bf16[448,2,128]{2,1,0:T(2,128)(2,1)}), bf16[3584,2,128]{2,1,0:T(2,128)(2,1)}) %all-gather.8.cloned.1.call-update) | async-done | bytes 1835024 | tf_op jit(solution)/shard_map/all_gather | solution.py:60
  234.5 7.2 %fusion.22 = f32[1536,256]{1,0:T(8,128)S(1)} fusion(bf16[1536,3584]{1,0:T(8,128)(2,1)} %bitcast.85, bf16[448,8,2,128]{3,2,1,0:T(2,128)(2,1)} %bitcast.94), kind=kOutput, calls=%fused_computation.34 | convolution fusion | flops 2818572288 | bytes 14417920 | tf_op jit(solution)/shard_map/dot_general | solution.py:64
  242.3 1.5 slice-done.1
  243.8 11.6 %fusion.4 = f32[32,48,7,128]{3,1,2,0:T(8,128)S(1)} fusion(bf16[7,128,3584,1]{2,1,0,3:T(8,128)(2,1)S(1)} %bitcast.90, bf16[32,48,3584]{2,1,0:T(8,128)(2,1)S(1)} %copy-done), kind=kOutput, calls=%fused_computation.7 | convolution fusion | flops 9865003008 | bytes 22937600 | tf_op jit(solution)/shard_map/dot_general | solution.py:63
  255.4 1.9 subtract_convert_fusion
  257.3 3.6 fusion.9
  261.0 2.1 fusion.8
  263.1 2.3 fusion.7
  265.4 70.8 %all-gather.12.cloned.1.call-done = bf16[896,3584]{0,1:T(8,128)(2,1)} async-done(((bf16[896,448]{0,1:T(8,128)(2,1)}), bf16[896,3584]{0,1:T(8,128)(2,1)}) %all-gather.12.cloned.1.call-update) | async-done | bytes 6422544 | tf_op jit(solution)/shard_map/all_gather | solution.py:86
  336.2 4.8 %convolution_convert_fusion.1 = bf16[32,3584]{1,0:T(8,128)(2,1)S(1)} fusion(bf16[896,3584]{0,1:T(8,128)(2,1)} %all-gather.12.cloned.1.call-done, f32[4,8,7,128]{3,2,1,0:T(8,128)S(1)} %bitcast.93, f32[32]{0:T(128)S(1)} %convert_element_type.93), kind=kOutput, calls=%fused_computation.20 | convolution fusion | flops 205692928 | bytes 6766720 | tf_op jit(solution)/shard_map/dot_general | solution.py:84
  341.1 9.3 %all-gather = bf16[128,3584]{1,0:T(8,128)(2,1)S(1)} all-gather(bf16[32,3584]{1,0:T(8,128)(2,1)S(1)} %convolution_convert_fusion.1), channel_id=2, replica_groups=mesh['dp'=8,'mp'=4] {'mp'}, dimensions={0}, use_global_device_ids=true | all-gather | bytes 1146880 | tf_op jit(solution)/shard_map/all_gather | solution.py:89
  350.8 1.0 convolution_convert_fusion
  351.8 3.4 all-to-all-start
  356.5 7.8 %all-to-all-done = bf16[8,4,3584]{2,1,0:T(4,128)(2,1)S(1)} async-done(((bf16[8,4,3584]{2,1,0:T(4,128)(2,1)}), bf16[8,4,3584]{2,1,0:T(4,128)(2,1)S(1)}, u32[]{:S(2)}, u32[]{:S(2)}) %all-to-all-start) | async-done | bytes 229408 | tf_op jit(solution)/shard_map/all_to_all | solution.py:121
  364.4 3.2 fusion.33
  367.6 9.8 %all_to_all.10 = bf16[8,4,512]{2,1,0:T(4,128)(2,1)S(1)} all-to-all(bf16[8,4,512]{2,1,0:T(4,128)(2,1)S(1)} %fusion.33), channel_id=1, replica_groups=mesh['dp'=8,'mp'=4] {'dp'}, dimensions={0} | all-to-all | bytes 65536 | tf_op jit(solution)/shard_map/all_to_all | solution.py:128
  377.4 0.8 convolution_bitcast_fusion
  (42 shorter events, 7.8 us)
Async XLA Ops:
  6.5 106.4 %all-gather.10.cloned.1.call-start = ((), (), s32[]{:S(2)}) async-start(), calls=%async_computation.4 | async-start | bytes 7225344 | tf_op jit(solution)/shard_map/all_gather | solution.py:59
  7.3 178.5 %all-gather.6.cloned.1.call-start = ((), (), s32[]{:S(2)}) async-start(), calls=%async_computation.2 | async-start | bytes 13762560 | tf_op jit(solution)/shard_map/all_gather | solution.py:49
  8.0 226.5 %all-gather.8.cloned.1.call-start = ((), (), s32[]{:S(2)}) async-start(), calls=%async_computation.3 | async-start | bytes 2064384 | tf_op jit(solution)/shard_map/all_gather | solution.py:60
  8.7 327.5 %all-gather.12.cloned.1.call-start = ((), (), s32[]{:S(2)}) async-start(), calls=%async_computation.5 | async-start | bytes 7225344 | tf_op jit(solution)/shard_map/all_gather | solution.py:86
  185.8 8.9 %copy-start.1 = (f32[3584]{0:T(1024)S(1)}, f32[3584]{0:T(1024)}, u32[]{:S(2)}) copy-start(f32[3584]{0:T(1024)} %param.12) | copy-start | bytes 43012
  194.7 47.4 %slice-start = ((s8[6422528]{0:T(1024)(128)(4,1)}), s8[2228224]{0:T(1024)(128)(4,1)S(1)}, s32[]{:S(2)}) async-start(s8[6422528]{0:T(1024)(128)(4,1)} %bitcast.88), calls=%async_computation.6 | async-start | bytes 4456448
  234.5 7.8 %copy-start = (bf16[32,48,3584]{2,1,0:T(8,128)(2,1)S(1)}, bf16[32,48,3584]{2,1,0:T(8,128)(2,1)}, u32[]{:S(2)}) copy-start(bf16[32,48,3584]{2,1,0:T(8,128)(2,1)} %fusion.3) | copy-start | bytes 33030148
  234.5 9.3 %slice-start.1 = ((s8[6422528]{0:T(1024)(128)(4,1)}), s8[4194304]{0:T(1024)(128)(4,1)S(1)}, s32[]{:S(2)}) async-start(s8[6422528]{0:T(1024)(128)(4,1)} %bitcast.88), calls=%async_computation.7 | async-start | bytes 8388608
  336.2 19.0 %copy-start.2 = (s32[8]{0:T(128)S(1)}, s32[8]{0:T(128)}, u32[]{:S(2)}) copy-start(s32[8]{0:T(128)} %param.19) | copy-start | bytes 100
  336.2 19.0 %copy-start.3 = (s32[8]{0:T(128)S(1)}, s32[8]{0:T(128)}, u32[]{:S(2)}) copy-start(s32[8]{0:T(128)} %param.20) | copy-start | bytes 100
  351.8 12.6 %all-to-all-start = ((bf16[8,4,3584]{2,1,0:T(4,128)(2,1)}), bf16[8,4,3584]{2,1,0:T(4,128)(2,1)S(1)}, u32[]{:S(2)}, u32[]{:S(2)}) async-start(bf16[8,4,3584]{2,1,0:T(4,128)(2,1)} %convolution_convert_fusion), calls=%async_computation | async-start | bytes 458752 | tf_op jit(solution)/shard_map/all_to_all | solution.py:121
Sparse Core Ops, SparseCore 0:
  9.5 103.3 all-gather.9
  114.5 71.2 all-gather.5
  188.0 46.4 all-gather.7
  236.5 99.6 all-gather.11
